TPU v7x, 512 devices: a whole 4x4x16 slice. The times are simulated.
512 devices in a mesh: freq: 32 (over x, z_hi, core), skel: 16 (over z_lo, y).
Axes of the slice: x: 4, y: 4, z: 16 (z_hi: 4, z_lo: 4; z = z_hi * 4 + z_lo), core: 2. Of those that a mesh axis runs over, the one named last changes fastest.
Arguments:
- incident: bfloat16 [32, 32768, 128], P('freq', 'skel'), may hold values from -6 to 6
- compress: bfloat16 [32, 32768, 128], P('freq', 'skel'), may hold values from -0.125 to 0.125
- coupling: bfloat16 [32, 2, 2048, 2048], P('freq', None, None, 'skel'), may hold values from -0.125 to 0.125
- expand: bfloat16 [32, 32768, 128], P('freq', 'skel'), may hold values from -0.5 to 0.5
- box_list: int32 [32], replicated, may hold values from 0 to 31, each once
- spectrum: float32 [32], replicated, may hold values from 0.1 to 0.4
Outputs:
- pulse: bfloat16 [32768, 64, 256], P(('skel', 'freq'))
Inputs may be any that keep to these rules, and one draw needn't show every extreme that they name: box_list names every box once.
All inputs are finite; a program needn't handle non-finite values.
Results may differ from a plain program's by a relative error of at most 0.007.
Values may be sent and summed in bfloat16 or wider, within the bound.
No kernel may reach another device: no remote copies, remote signals or barrier semaphores. Data moves between devices by JAX's collectives and lax.ppermute only.
A program may use at most 64 MiB of HBM per device.

v0:
```python
import math

import jax
import jax.numpy as jnp
from jax import lax
from jax.sharding import PartitionSpec as P

BOX = 1024
NT = 2048
FREQ_LOW = 640
TWIN = 256


def stack_complex(values, angles):
    real_part = values[..., :angles]
    imag_part = values[..., angles:]
    top = jnp.concatenate([real_part, imag_part], axis=-1)
    bottom = jnp.concatenate([-imag_part, real_part], axis=-1)
    return jnp.concatenate([top, bottom], axis=-2)


def time_traces(spaced, dft_table, angles):
    all_freqs = spaced.shape[0]
    strip_rows = spaced.shape[1]
    return jnp.einsum(
        "fnca,cft->nat",
        spaced.reshape(all_freqs, strip_rows, 2, angles),
        dft_table,
        preferred_element_type=jnp.float32,
    )


def on_device(incident, compress, coupling, expand, box_list, spectrum):
    freq_dev = incident.shape[0]
    local_rows = incident.shape[1]
    columns = incident.shape[2]
    angles = columns // 2
    rank_cols = compress.shape[2]
    skel_rank = rank_cols // 2
    box_count = local_rows // BOX
    local_skel = box_count * skel_rank
    all_boxes = coupling.shape[2] // skel_rank
    product = jnp.einsum(
        "fkxr,fkxa->fkra",
        compress.reshape(freq_dev, box_count, BOX, rank_cols),
        incident.reshape(freq_dev, box_count, BOX, columns),
        preferred_element_type=jnp.float32,
    )
    real_part = product[:, :, :skel_rank, :angles] - product[:, :, skel_rank:, angles:]
    imag_part = product[:, :, :skel_rank, angles:] + product[:, :, skel_rank:, :angles]
    compressed = jnp.concatenate([real_part, imag_part], axis=-1).astype(jnp.bfloat16)
    compressed = compressed.reshape(freq_dev, local_skel, columns)
    matrix = coupling.reshape(freq_dev, 2, all_boxes, skel_rank, local_skel)
    picked = jnp.take(matrix, box_list, axis=2)
    halves = jnp.einsum("fpbrk,fka->pbfra", picked, compressed, preferred_element_type=jnp.float32)
    summed_real = halves[0, ..., :angles] - halves[1, ..., angles:]
    summed_imag = halves[0, ..., angles:] + halves[1, ..., :angles]
    owned = lax.psum_scatter(
        jnp.concatenate([summed_real, summed_imag], axis=-1),
        "skel",
        scatter_dimension=0,
        tiled=True,
    ).astype(jnp.bfloat16)
    stacked = stack_complex(owned, angles)
    factors = expand.reshape(freq_dev, box_count, BOX, rank_cols)
    all_freqs = spectrum.shape[0]
    freq_index = jnp.arange(all_freqs, dtype=jnp.int32) + FREQ_LOW
    time_index = jnp.arange(TWIN, dtype=jnp.int32)
    phases = (freq_index[:, None] * time_index[None, :] % NT).astype(jnp.float32) * (
        2.0 * math.pi / NT
    )
    weights = spectrum[:, None]
    dft_table = jnp.stack([weights * jnp.cos(phases), -weights * jnp.sin(phases)]).astype(
        jnp.bfloat16
    )
    response = jnp.einsum("fkxr,kfra->fkxa", factors, stacked, preferred_element_type=jnp.float32)
    response = response.astype(jnp.bfloat16).reshape(freq_dev, local_rows, columns)
    spaced = lax.all_to_all(response, "freq", split_axis=1, concat_axis=0, tiled=True)
    traces = time_traces(spaced, dft_table, angles)
    return traces.astype(jnp.bfloat16)


def solution(mesh):
    placed = (
        P("freq", "skel", None),
        P("freq", "skel", None),
        P("freq", None, None, "skel"),
        P("freq", "skel", None),
        P(),
        P(),
    )
    return jax.shard_map(
        on_device,
        mesh=mesh,
        in_specs=placed,
        out_specs=P(("skel", "freq"), None, None),
        check_vma=False,
    )
```

profile of v0, /device:TPU:9, one launch (start us, length us, event | category | flops | bytes accessed | tf_op | source)
XLA Modules:
  0.0 187.6 jit_solution(12249212706682702324)
XLA Ops:
  6.5 0.0 copy-start
  6.5 0.0 reduce-scatter.2.cloned.1.call-start
  6.5 0.7 compare_select_fusion
  7.3 0.7 compare_and_fusion
  7.9 1.5 convolution_bitcast_fusion
  9.5 0.1 fusion.7
  9.6 0.0 copy-done
  9.6 0.7 gather_fusion
  10.4 0.5 fusion.4
  10.9 0.3 fusion.1
  11.2 0.3 fusion.2
  11.6 0.0 copy-start.1
  11.6 1.3 pad_maximum_fusion
  12.9 0.0 reduce-scatter.2.cloned.1.call-update
  12.9 80.2 %reduce-scatter.2.cloned.1.call-done = f32[2,1,64,128]{3,2,0,1:T(8,128)} async-done(((f32[32,1,64,128]{3,2,0,1:T(8,128)}), f32[2,1,64,128]{3,2,0,1:T(8,128)}) %reduce-scatter.2.cloned.1.call-update) | async-done | bytes 65552 | tf_op jit(solution)/shard_map/reduce_scatter | solution.py:58
  93.2 0.8 convert_element_type.35
  94.0 0.1 slice_negate_fusion
  94.1 0.0 copy-done.1
  94.1 0.4 fusion
  94.5 0.3 copy.24
  94.8 8.1 %copy.39 = bf16[1,2048,128]{2,0,1:T(2,128)(2,1)S(1)} copy(bf16[1,2048,128]{2,1,0:T(8,128)(2,1)S(1)} %bitcast.51) | data formatting | bytes 1048576 | tf_op jit(solution)/shard_map/reshape | solution.py:77
  102.9 0.0 copy-start.2
  102.9 0.5 broadcast.166
  103.5 11.5 %reduce.2 = bf16[2048,128]{1,0:T(8,128)(2,1)S(1)} reduce(bf16[2048,1,128]{2,1,0:T(2,128)(2,1)S(1)} %bitcast.50, bf16[]{:T(256)} %broadcast.166), dimensions={1}, to_apply=%bitcast.46.reduce_sub_computation | reduce | bytes 1048578
  115.0 0.9 reshape.275
  115.9 26.3 %all-to-all-start = ((bf16[32,2,4096]{2,1,0:T(2,128)(2,1)}), bf16[32,2,4096]{2,1,0:T(2,128)(2,1)S(1)}, u32[]{:S(2)}, u32[]{:S(2)}) async-start(bf16[32,2,4096]{2,1,0:T(2,128)(2,1)} %reshape.275), calls=%async_computation.1 | async-start | bytes 1048576 | tf_op jit(solution)/shard_map/all_to_all | solution.py:78
  142.2 0.0 copy-done.2
  142.2 0.2 multiply_convert_fusion.1
  142.5 26.2 %all-to-all-done = bf16[32,2,4096]{2,1,0:T(2,128)(2,1)S(1)} async-done(((bf16[32,2,4096]{2,1,0:T(2,128)(2,1)}), bf16[32,2,4096]{2,1,0:T(2,128)(2,1)S(1)}, u32[]{:S(2)}, u32[]{:S(2)}) %all-to-all-start) | async-done | bytes 524320 | tf_op jit(solution)/shard_map/all_to_all | solution.py:78
  168.6 0.5 reshape.276
  169.2 8.8 %bitcast_reduce_fusion = bf16[2048,128]{1,0:T(8,128)(2,1)S(1)} fusion(bf16[2048,1,128]{2,1,0:T(2,128)(2,1)S(1)} %reshape.276), kind=kLoop, calls=%fused_computation.48 | loop fusion | bytes 1048576 | tf_op jit(solution)/shard_map/all_to_all | solution.py:78
  177.9 0.4 reshape.273
  178.3 2.5 %bitcast_convert_fusion = bf16[64,64,256]{2,1,0:T(8,128)(2,1)} fusion(bf16[32,64,2,64]{3,2,1,0:T(2,128)(2,1)S(1)} %reshape.273, bf16[1,32,256]{2,1,0:T(8,128)(2,1)S(1)} %get-tuple-element.10, bf16[1,32,256]{2,1,0:T(8,128)(2,1)S(1)} %get-tuple-element.9), kind=kOutput, calls=%fused_computation.1 | convolution fusion | flops 135282688 | bytes 2654208 | tf_op jit(solution)/shard_map/fnca,cft->nat/dot_general | solution.py:25
  (3 shorter events, 0.0 us)
Async XLA Ops:
  6.5 3.1 %copy-start = (bf16[1,2,2048,128]{3,2,1,0:T(8,128)(2,1)S(1)}, bf16[1,2,2048,128]{3,2,1,0:T(8,128)(2,1)}, u32[]{:S(2)}) copy-start(bf16[1,2,2048,128]{3,2,1,0:T(8,128)(2,1)} %param.8) | copy-start | bytes 3145732
  6.5 86.6 %reduce-scatter.2.cloned.1.call-start = ((), (), s32[]{:S(2)}) async-start(), calls=%async_computation.2 | async-start | bytes 1114112 | tf_op jit(solution)/shard_map/reduce_scatter | solution.py:58
  11.6 82.5 %copy-start.1 = (bf16[1,2048,128]{2,1,0:T(8,128)(2,1)S(1)}, bf16[1,2048,128]{2,1,0:T(8,128)(2,1)}, u32[]{:S(2)}) copy-start(bf16[1,2048,128]{2,1,0:T(8,128)(2,1)} %param.9) | copy-start | bytes 1572868
  102.9 39.3 %copy-start.2 = (f32[32]{0:T(128)S(1)}, f32[32]{0:T(128)}, u32[]{:S(2)}) copy-start(f32[32]{0:T(128)} %param.11) | copy-start | bytes 388
  115.9 52.7 %all-to-all-start = ((bf16[32,2,4096]{2,1,0:T(2,128)(2,1)}), bf16[32,2,4096]{2,1,0:T(2,128)(2,1)S(1)}, u32[]{:S(2)}, u32[]{:S(2)}) async-start(bf16[32,2,4096]{2,1,0:T(2,128)(2,1)} %reshape.275), calls=%async_computation.1 | async-start | bytes 1048576 | tf_op jit(solution)/shard_map/all_to_all | solution.py:78
Sparse Core Ops, SparseCore 0:
  13.0 80.0 reduce-scatter.1
where the time goes:
time: 188 us
  waiting for transfers between devices  106 us (56%)
  starting transfers between devices  26.3 us (14%)
  local copies, waits for them, and re-layouts  20.3 us (11%)
  other arithmetic  16.2 us (9%)
  between operations  13.6 us (7%)
  matrix products  4.9 us (3%)
    reduce_scatter x1, waiting for transfers between devices, on_device(): lax.psum_scatter(jnp.concatenate([summed_real, summed_imag], axis=-1), 's...  80.2 us
    all_to_all x1, starting transfers between devices, on_device(): lax.all_to_all(response, 'freq', split_axis=1, concat_axis=0, tiled=True)  26.3 us
    all_to_all x1, waiting for transfers between devices, on_device(): lax.all_to_all(response, 'freq', split_axis=1, concat_axis=0, tiled=True)  26.2 us
    unnamed x1, other arithmetic  11.5 us
    all_to_all x1, local copies, waits for them, and re-layouts, on_device(): lax.all_to_all(response, 'freq', split_axis=1, concat_axis=0, tiled=True)  8.76 us
    reshape x1, local copies, waits for them, and re-layouts, on_device(): response.astype(jnp.bfloat16).reshape(freq_dev, local_rows, columns)  8.14 us
  transfers between devices with their start and end apart: 2, of which 2 were waited for; matrix products, arithmetic and copies ran while one was open for 0% of the time, Pallas kernels for 0%

commit v1 on v0

v1 whole, which is shorter than its diff:
```python
import math

import jax
import jax.numpy as jnp
from jax import lax
from jax.sharding import PartitionSpec as P

BOX = 1024
NT = 2048
FREQ_LOW = 640
TWIN = 256


def time_table(spectrum):
    all_freqs = spectrum.shape[0]
    freq_index = jnp.arange(all_freqs, dtype=jnp.int32) + FREQ_LOW
    time_index = jnp.arange(TWIN, dtype=jnp.int32)
    phases = (freq_index[:, None] * time_index[None, :] % NT).astype(jnp.float32) * (
        2.0 * math.pi / NT
    )
    weights = spectrum[:, None]
    return jnp.stack([weights * jnp.cos(phases), -weights * jnp.sin(phases)]).astype(
        jnp.bfloat16
    )


def turned(values, angles):
    return jnp.concatenate([-values[..., angles:], values[..., :angles]], axis=-1)


def on_device(incident, compress, coupling, expand, box_list, spectrum, *, freqs, skels):
    local_rows, columns = incident.shape[1:]
    angles = columns // 2
    rank_cols = compress.shape[2]
    rank = rank_cols // 2
    boxes = local_rows // BOX
    product = jnp.einsum(
        "kxr,kxa->kra",
        compress.reshape(boxes, BOX, rank_cols),
        incident.reshape(boxes, BOX, columns),
        preferred_element_type=jnp.float32,
    )
    compressed = product[:, :rank] + turned(product[:, rank:], angles)
    compressed = compressed.astype(jnp.bfloat16).reshape(boxes * rank, columns)
    both = jnp.stack([compressed, turned(compressed, angles)])
    all_boxes = coupling.shape[2] // rank
    partial = jnp.einsum(
        "pmk,pka->ma", coupling[0], both, preferred_element_type=jnp.float32
    ).astype(jnp.bfloat16)
    picked = jnp.take(partial.reshape(all_boxes, rank * columns // 128, 128), box_list, axis=0)
    sent = picked.reshape(skels, boxes * rank, columns)
    parts = lax.all_to_all(sent, "skel", split_axis=0, concat_axis=0, tiled=True)
    owned = jnp.sum(parts.astype(jnp.float32), axis=0).astype(jnp.bfloat16)
    owned = owned.reshape(boxes, rank, columns)
    stacked = jnp.concatenate([owned, turned(owned, angles)], axis=1)
    response = jnp.einsum(
        "kxr,kra->kxa",
        expand.reshape(boxes, BOX, rank_cols),
        stacked,
        preferred_element_type=jnp.float32,
    ).astype(jnp.bfloat16)
    response = response.reshape(freqs, local_rows // freqs, columns)
    spaced = lax.all_to_all(response, "freq", split_axis=0, concat_axis=0, tiled=True)
    traces = jnp.einsum(
        "fnca,cft->nat",
        spaced.reshape(freqs, local_rows // freqs, 2, angles),
        time_table(spectrum),
        preferred_element_type=jnp.float32,
    )
    return traces.astype(jnp.bfloat16)


def solution(mesh):
    placed = (
        P("freq", "skel", None),
        P("freq", "skel", None),
        P("freq", None, None, "skel"),
        P("freq", "skel", None),
        P(),
        P(),
    )

    def body(*args):
        return on_device(*args, freqs=mesh.shape["freq"], skels=mesh.shape["skel"])

    return jax.shard_map(
        body,
        mesh=mesh,
        in_specs=placed,
        out_specs=P(("skel", "freq"), None, None),
        check_vma=False,
    )
```

time: 188 us -> 83.8 us (0.45)
  the two profiles are of different devices: /device:TPU:9 before, /device:TPU:33 now
where the time goes in v1:
time: 83.8 us; the launch traced here: 83.5 us
  waiting for transfers between devices  34.3 us (41%)
  blocking collectives  21.9 us (26%)
  starting transfers between devices  17.1 us (20%)
  matrix products  4.8 us (6%)
  local copies, waits for them, and re-layouts  3.09 us (4%)
  other arithmetic  2.24 us (3%)
    all_to_all x1, waiting for transfers between devices, on_device(): lax.all_to_all(response, 'freq', split_axis=0, concat_axis=0, tiled=True)  34.3 us
    all_to_all x1, blocking collectives, on_device(): lax.all_to_all(sent, 'skel', split_axis=0, concat_axis=0, tiled=True)  21.9 us
    all_to_all x1, starting transfers between devices, on_device(): lax.all_to_all(response, 'freq', split_axis=0, concat_axis=0, tiled=True)  17.1 us
    dot_general x1, matrix products, on_device(): jnp.einsum('fnca,cft->nat', spaced.reshape(freqs, local_rows // freqs, 2,...  2.44 us
  transfers between devices with their start and end apart: 1, of which 1 were waited for; matrix products, arithmetic and copies ran while one was open for 0% of the time, Pallas kernels for 0%

profile of v1, /device:TPU:33, one launch (start us, length us, event | category | flops | bytes accessed | tf_op | source)
XLA Modules:
  0.0 83.5 jit_solution(8331218631309658264)
XLA Ops:
  0.0 0.0 copy-start
  0.0 0.8 compare_and_fusion
  0.8 0.7 compare_select_fusion
  1.4 0.1 broadcast_in_dim.21
  1.5 0.1 broadcast_in_dim.22
  1.6 0.1 broadcast_in_dim.23
  1.7 1.5 %fusion.26 = f32[2,128,128]{2,1,0:T(8,128)S(1)} fusion(bf16[2,1024,128]{2,1,0:T(8,128)(2,1)} %bitcast.39, bf16[2,1024,128]{2,1,0:T(8,128)(2,1)} %bitcast.40), kind=kOutput, calls=%fused_computation.45 | convolution fusion | flops 67108864 | bytes 1179648 | tf_op jit(solution)/shard_map/kxr,kxa->kra/dot_general | solution.py:37
  3.2 0.1 slice_negate_fusion
  3.3 0.1 fusion.5
  3.4 0.1 copy.14
  3.5 0.1 fusion.25
  3.6 0.1 copy.23
  3.7 0.1 copy.24
  3.9 0.0 copy-done
  3.9 0.5 fusion.1
  4.3 0.3 copy.15
  4.6 0.0 copy-start.1
  4.6 0.6 gather_fusion
  5.3 0.3 bitcast_select_fusion
  5.6 21.9 %all_to_all.10 = bf16[16,128,128]{2,1,0:T(8,128)(2,1)S(1)} all-to-all(bf16[16,128,128]{2,1,0:T(8,128)(2,1)S(1)} %bitcast_select_fusion), channel_id=1, replica_groups=mesh['freq'=32,'skel'=16] {'skel'}, dimensions={0} | all-to-all | bytes 1048576 | tf_op jit(solution)/shard_map/all_to_all | solution.py:52
  27.5 0.0 copy-start.2
  27.5 0.1 reduce_sum.12
  27.6 0.1 copy.18
  27.7 0.0 copy-done.1
  27.7 0.3 fusion.2
  28.1 1.0 %copy.19 = bf16[2,1024,128]{2,1,0:T(8,128)(2,1)} copy(bf16[2,1024,128]{1,2,0:T(8,128)(2,1)S(1)} %fusion.2) | data formatting | bytes 1048576 | tf_op jit(solution)/shard_map/convert_element_type | solution.py:61
  29.1 17.1 %all-to-all-start.1 = ((bf16[32,64,128]{2,1,0:T(8,128)(2,1)}), bf16[32,64,128]{2,1,0:T(8,128)(2,1)S(1)}, u32[]{:S(2)}, u32[]{:S(2)}) async-start(bf16[32,64,128]{2,1,0:T(8,128)(2,1)} %bitcast.13), calls=%async_computation.1 | async-start | bytes 1048576 | tf_op jit(solution)/shard_map/all_to_all | solution.py:63
  46.2 0.0 copy-done.2
  46.2 0.2 multiply_convert_fusion.1
  46.4 34.3 %all-to-all-done.1 = bf16[32,64,128]{2,1,0:T(8,128)(2,1)S(1)} async-done(((bf16[32,64,128]{2,1,0:T(8,128)(2,1)}), bf16[32,64,128]{2,1,0:T(8,128)(2,1)S(1)}, u32[]{:S(2)}, u32[]{:S(2)}) %all-to-all-start.1) | async-done | bytes 524320 | tf_op jit(solution)/shard_map/all_to_all | solution.py:63
  80.7 0.4 reshape.186
  81.1 2.4 %bitcast_convert_fusion = bf16[64,64,256]{2,1,0:T(8,128)(2,1)} fusion(bf16[32,64,2,64]{3,2,1,0:T(2,128)(2,1)S(1)} %reshape.186, bf16[1,32,256]{2,1,0:T(8,128)(2,1)S(1)} %get-tuple-element.12, bf16[1,32,256]{2,1,0:T(8,128)(2,1)S(1)} %get-tuple-element.11), kind=kOutput, calls=%fused_computation.1 | convolution fusion | flops 135282688 | bytes 2654208 | tf_op jit(solution)/shard_map/fnca,cft->nat/dot_general | solution.py:64
  (6 shorter events, 0.0 us)
Async XLA Ops:
  0.0 3.9 %copy-start = (bf16[1,2,2048,128]{3,2,1,0:T(8,128)(2,1)S(1)}, bf16[1,2,2048,128]{3,2,1,0:T(8,128)(2,1)}, u32[]{:S(2)}) copy-start(bf16[1,2,2048,128]{3,2,1,0:T(8,128)(2,1)} %param.8) | copy-start | bytes 3145732
  4.6 23.1 %copy-start.1 = (bf16[1,2048,128]{2,1,0:T(8,128)(2,1)S(1)}, bf16[1,2048,128]{2,1,0:T(8,128)(2,1)}, u32[]{:S(2)}) copy-start(bf16[1,2048,128]{2,1,0:T(8,128)(2,1)} %param.9) | copy-start | bytes 1572868
  27.5 18.7 %copy-start.2 = (f32[32]{0:T(128)S(1)}, f32[32]{0:T(128)}, u32[]{:S(2)}) copy-start(f32[32]{0:T(128)} %param.11) | copy-start | bytes 388
  29.1 51.6 %all-to-all-start.1 = ((bf16[32,64,128]{2,1,0:T(8,128)(2,1)}), bf16[32,64,128]{2,1,0:T(8,128)(2,1)S(1)}, u32[]{:S(2)}, u32[]{:S(2)}) async-start(bf16[32,64,128]{2,1,0:T(8,128)(2,1)} %bitcast.13), calls=%async_computation.1 | async-start | bytes 1048576 | tf_op jit(solution)/shard_map/all_to_all | solution.py:63

commit v2 on v1

v2 whole, which is shorter than its diff:
```python
import functools
import math

import jax
import jax.numpy as jnp
from jax import lax
from jax.experimental import pallas as pl
from jax.experimental.pallas import tpu as pltpu
from jax.sharding import PartitionSpec as P

BOX = 1024
NT = 2048
FREQ_LOW = 640
TWIN = 256
CHUNK = 256
SMALL_GRANT = 12 << 20


def time_table(spectrum):
    all_freqs = spectrum.shape[0]
    freq_index = jnp.arange(all_freqs, dtype=jnp.int32) + FREQ_LOW
    time_index = jnp.arange(TWIN, dtype=jnp.int32)
    phases = (freq_index[:, None] * time_index[None, :] % NT).astype(jnp.float32) * (
        2.0 * math.pi / NT
    )
    weights = spectrum[:, None]
    return jnp.stack([weights * jnp.cos(phases), -weights * jnp.sin(phases)]).astype(
        jnp.bfloat16
    )


def turned(values):
    columns = values.shape[-1]
    swapped = pltpu.roll(values, columns // 2, 1)
    lane = lax.broadcasted_iota(jnp.int32, values.shape, 1)
    return jnp.where(lane < columns // 2, -swapped, swapped)


def front_kernel(boxes, rank, box_ref, compress_ref, incident_ref, coupling_ref, sent_ref, place_ref):
    all_boxes = box_ref.shape[0]
    for position in range(all_boxes):
        place_ref[box_ref[position]] = position
    plain, other = [], []
    for k in range(boxes):
        rows = pl.ds(k * BOX, BOX)
        product = lax.dot_general(
            compress_ref[rows, :],
            incident_ref[rows, :],
            (((0,), (0,)), ((), ())),
            preferred_element_type=jnp.float32,
        )
        compressed = product[:rank] + turned(product[rank:])
        compressed = compressed.astype(jnp.bfloat16).astype(jnp.float32)
        plain.append(compressed)
        other.append(turned(compressed))
    both = jnp.concatenate(plain + other, axis=0).astype(jnp.bfloat16)
    for start in range(0, all_boxes * rank, CHUNK):
        rows = pl.ds(start, CHUNK)
        matrix = jnp.concatenate([coupling_ref[0, rows, :], coupling_ref[1, rows, :]], axis=1)
        partial = jnp.dot(matrix, both, preferred_element_type=jnp.float32).astype(jnp.bfloat16)
        for part in range(CHUNK // rank):
            target = pl.multiple_of(place_ref[start // rank + part] * rank, rank)
            sent_ref[pl.ds(target, rank), :] = partial[part * rank : (part + 1) * rank]


def mid_kernel(boxes, rank, parts_ref, expand_ref, response_ref):
    total = parts_ref[0].astype(jnp.float32)
    for source in range(1, parts_ref.shape[0]):
        total = total + parts_ref[source].astype(jnp.float32)
    total = total.astype(jnp.bfloat16).astype(jnp.float32)
    for k in range(boxes):
        owned = total[k * rank : (k + 1) * rank]
        stacked = jnp.concatenate([owned, turned(owned)], axis=0).astype(jnp.bfloat16)
        for start in range(k * BOX, (k + 1) * BOX, CHUNK):
            rows = pl.ds(start, CHUNK)
            response_ref[rows, :] = jnp.dot(
                expand_ref[rows, :], stacked, preferred_element_type=jnp.float32
            ).astype(jnp.bfloat16)


def on_device(incident, compress, coupling, expand, box_list, spectrum, *, freqs, skels):
    local_rows, columns = incident.shape[1:]
    angles = columns // 2
    rank = compress.shape[2] // 2
    boxes = local_rows // BOX
    all_rows = coupling.shape[2]
    vmem = pl.BlockSpec(memory_space=pltpu.VMEM)
    sent = pl.pallas_call(
        functools.partial(front_kernel, boxes, rank),
        out_shape=jax.ShapeDtypeStruct((all_rows, columns), jnp.bfloat16),
        in_specs=[pl.BlockSpec(memory_space=pltpu.SMEM), vmem, vmem, vmem],
        out_specs=vmem,
        scratch_shapes=[pltpu.SMEM((all_rows // rank,), jnp.int32)],
        name="front",
    )(box_list, compress[0], incident[0], coupling[0])
    sent = sent.reshape(skels, all_rows // skels, columns)
    parts = lax.all_to_all(sent, "skel", split_axis=0, concat_axis=0, tiled=True)
    response = pl.pallas_call(
        functools.partial(mid_kernel, boxes, rank),
        out_shape=jax.ShapeDtypeStruct((local_rows, columns), jnp.bfloat16),
        in_specs=[vmem, vmem],
        out_specs=vmem,
        name="mid", compiler_params=pltpu.CompilerParams(vmem_limit_bytes=SMALL_GRANT),
    )(parts, expand[0])
    response = response.reshape(freqs, local_rows // freqs, columns)
    spaced = lax.all_to_all(response, "freq", split_axis=0, concat_axis=0, tiled=True)
    traces = jnp.einsum(
        "fnca,cft->nat",
        spaced.reshape(freqs, local_rows // freqs, 2, angles),
        time_table(spectrum),
        preferred_element_type=jnp.float32,
    )
    return traces.astype(jnp.bfloat16)


def solution(mesh):
    placed = (
        P("freq", "skel", None),
        P("freq", "skel", None),
        P("freq", None, None, "skel"),
        P("freq", "skel", None),
        P(),
        P(),
    )

    def body(*args):
        return on_device(*args, freqs=mesh.shape["freq"], skels=mesh.shape["skel"])

    return jax.shard_map(
        body,
        mesh=mesh,
        in_specs=placed,
        out_specs=P(("skel", "freq"), None, None),
        check_vma=False,
    )
```

time: 83.8 us -> 81.5 us (0.973)
  Pallas kernels: 0 us -> 4.47 us
  local copies, waits for them, and re-layouts: 3.09 us -> 0.41 us
  matrix products: 4.8 us -> 2.45 us
  other arithmetic: 2.24 us -> 0.22 us
    pallas_call x0 -> x2, Pallas kernels: none -> 4.47 us  [the longest x1 3.29 us: on_device(): pl.pallas_call(functools.partial(front_kernel, boxes, rank), out_shape=ja...]
    dot_general x3 -> x0, matrix products: 2.36 us -> none  [the longest x1 1.54 us: on_device(): jnp.einsum('kxr,kxa->kra', compress.reshape(boxes, BOX, rank_cols), incid...]
    convert_element_type x2 -> x0, local copies, waits for them, and re-layouts: 1.27 us -> none  [the longest x1 1 us: on_device(): response = jnp.einsum('kxr,kra->kxa', expand.reshape(boxes, BOX, rank_col...]
    select_n x2 -> x0, other arithmetic: 1 us -> none  [on_device(): jnp.take(partial.reshape(all_boxes, rank * columns // 128, 128), box_list...]
where the time goes in v2:
time: 81.5 us; the launch traced here: 81.1 us
  waiting for transfers between devices  34.3 us (42%)
  blocking collectives  22.2 us (27%)
  starting transfers between devices  17.1 us (21%)
  Pallas kernels  4.47 us (5%)
  matrix products  2.45 us (3%)
    all_to_all x1, waiting for transfers between devices, on_device(): lax.all_to_all(response, 'freq', split_axis=0, concat_axis=0, tiled=True)  34.3 us
    all_to_all x1, blocking collectives, on_device(): lax.all_to_all(sent, 'skel', split_axis=0, concat_axis=0, tiled=True)  22.2 us
    all_to_all x1, starting transfers between devices, on_device(): lax.all_to_all(response, 'freq', split_axis=0, concat_axis=0, tiled=True)  17.1 us
    pallas_call x1, Pallas kernels, on_device(): pl.pallas_call(functools.partial(front_kernel, boxes, rank), out_shape=ja...  3.29 us
    dot_general x1, matrix products, on_device(): jnp.einsum('fnca,cft->nat', spaced.reshape(freqs, local_rows // freqs, 2,...  2.45 us
  transfers between devices with their start and end apart: 1, of which 1 were waited for; matrix products, arithmetic and copies ran while one was open for 0% of the time, Pallas kernels for 0%

profile of v2, /device:TPU:33, one launch (start us, length us, event | category | flops | bytes accessed | tf_op | source)
XLA Modules:
  0.0 81.1 jit_solution(17059317456085634186)
XLA Ops:
  0.0 0.0 copy-start
  0.0 3.3 %front.1 = bf16[2048,128]{1,0:T(8,128)(2,1)} custom-call(s32[32]{0:T(128)} %box_ref.1, bf16[2048,128]{1,0:T(8,128)(2,1)} %bitcast.15, bf16[2048,128]{1,0:T(8,128)(2,1)} %bitcast.16, bf16[2,2048,128]{2,1,0:T(8,128)(2,1)} %bitcast.14), custom_call_target="tpu_custom_call" | custom-call | tf_op jit(solution)/shard_map/front/pallas_call | solution.py:88
  3.3 0.0 copy-start.1
  3.3 22.2 %all_to_all.10.parts_ref = bf16[16,128,128]{2,1,0:T(8,128)(2,1)S(1)} all-to-all(bf16[16,128,128]{2,1,0:T(8,128)(2,1)} %bitcast.13), channel_id=1, replica_groups=mesh['freq'=32,'skel'=16] {'skel'}, dimensions={0} | all-to-all | bytes 1048576 | tf_op jit(solution)/shard_map/all_to_all | solution.py:97
  25.5 0.0 copy-done
  25.5 1.2 %mid.1 = bf16[2048,128]{1,0:T(8,128)(2,1)} custom-call(bf16[16,128,128]{2,1,0:T(8,128)(2,1)S(1)} %all_to_all.10.parts_ref, bf16[2048,128]{1,0:T(8,128)(2,1)S(1)} %bitcast.12), custom_call_target="tpu_custom_call" | custom-call | tf_op jit(solution)/shard_map/mid/pallas_call | solution.py:98
  26.7 17.1 %all-to-all-start.1 = ((bf16[32,64,128]{2,1,0:T(8,128)(2,1)}), bf16[32,64,128]{2,1,0:T(8,128)(2,1)S(1)}, u32[]{:S(2)}, u32[]{:S(2)}) async-start(bf16[32,64,128]{2,1,0:T(8,128)(2,1)} %bitcast.5), calls=%async_computation.1 | async-start | bytes 1048576 | tf_op jit(solution)/shard_map/all_to_all | solution.py:106
  43.7 0.0 copy-done.1
  43.8 0.2 multiply_convert_fusion.1
  44.0 34.3 %all-to-all-done.1 = bf16[32,64,128]{2,1,0:T(8,128)(2,1)S(1)} async-done(((bf16[32,64,128]{2,1,0:T(8,128)(2,1)}), bf16[32,64,128]{2,1,0:T(8,128)(2,1)S(1)}, u32[]{:S(2)}, u32[]{:S(2)}) %all-to-all-start.1) | async-done | bytes 524320 | tf_op jit(solution)/shard_map/all_to_all | solution.py:106
  78.3 0.4 reshape.155
  78.7 2.4 %bitcast_convert_fusion = bf16[64,64,256]{2,1,0:T(8,128)(2,1)} fusion(bf16[32,64,2,64]{3,2,1,0:T(2,128)(2,1)S(1)} %reshape.155, bf16[1,32,256]{2,1,0:T(8,128)(2,1)S(1)} %get-tuple-element.6, bf16[1,32,256]{2,1,0:T(8,128)(2,1)S(1)} %get-tuple-element.5), kind=kOutput, calls=%fused_computation | convolution fusion | flops 135282688 | bytes 2654208 | tf_op jit(solution)/shard_map/fnca,cft->nat/dot_general | solution.py:107
  (2 shorter events, 0.0 us)
Async XLA Ops:
  0.0 25.5 %copy-start = (bf16[1,2048,128]{2,1,0:T(8,128)(2,1)S(1)}, bf16[1,2048,128]{2,1,0:T(8,128)(2,1)}, u32[]{:S(2)}) copy-start(bf16[1,2048,128]{2,1,0:T(8,128)(2,1)} %param.9) | copy-start | bytes 1572868
  3.3 40.4 %copy-start.1 = (f32[32]{0:T(128)S(1)}, f32[32]{0:T(128)}, u32[]{:S(2)}) copy-start(f32[32]{0:T(128)} %param.11) | copy-start | bytes 388
  26.7 51.6 %all-to-all-start.1 = ((bf16[32,64,128]{2,1,0:T(8,128)(2,1)}), bf16[32,64,128]{2,1,0:T(8,128)(2,1)S(1)}, u32[]{:S(2)}, u32[]{:S(2)}) async-start(bf16[32,64,128]{2,1,0:T(8,128)(2,1)} %bitcast.5), calls=%async_computation.1 | async-start | bytes 1048576 | tf_op jit(solution)/shard_map/all_to_all | solution.py:106

commit v3 on v2

--- a/solution.py
+++ b/solution.py
@@ -6,7 +6,7 @@
 from jax import lax
 from jax.experimental import pallas as pl
 from jax.experimental.pallas import tpu as pltpu
-from jax.sharding import PartitionSpec as P
+from jax.sharding import Mesh, PartitionSpec as P
 
 BOX = 1024
 NT = 2048
@@ -16,9 +16,42 @@
 SMALL_GRANT = 12 << 20
 
 
+FREQ_AXES = ("x", "far", "core")
+FREQ_SIZES = (4, 4, 2)
+FREQ_WALK = ("far", "core", "x")
+SKEL_AXES = ("near", "y")
+SKEL_SIZES = (4, 4)
+SKEL_WALK = ("y", "near")
+
+
+def walked(sizes, axes, walk):
+    members = []
+    for place in range(math.prod(sizes)):
+        at = {}
+        for axis in reversed(walk):
+            size = sizes[axes.index(axis)]
+            at[axis] = place % size
+            place //= size
+        member = 0
+        for axis, size in zip(axes, sizes):
+            member = member * size + at[axis]
+        members.append(member)
+    return members
+
+
+FREQ_ORDER = walked(FREQ_SIZES, FREQ_AXES, FREQ_WALK)
+SKEL_ORDER = walked(SKEL_SIZES, SKEL_AXES, SKEL_WALK)
+
+
+def in_walk(values):
+    axes = [FREQ_AXES.index(axis) for axis in FREQ_WALK]
+    return values.reshape(FREQ_SIZES).transpose(axes).reshape(-1)
+
+
 def time_table(spectrum):
     all_freqs = spectrum.shape[0]
-    freq_index = jnp.arange(all_freqs, dtype=jnp.int32) + FREQ_LOW
+    spectrum = in_walk(spectrum)
+    freq_index = in_walk(jnp.arange(all_freqs, dtype=jnp.int32)) + FREQ_LOW
     time_index = jnp.arange(TWIN, dtype=jnp.int32)
     phases = (freq_index[:, None] * time_index[None, :] % NT).astype(jnp.float32) * (
         2.0 * math.pi / NT
@@ -39,7 +72,8 @@
 def front_kernel(boxes, rank, box_ref, compress_ref, incident_ref, coupling_ref, sent_ref, place_ref):
     all_boxes = box_ref.shape[0]
     for position in range(all_boxes):
-        place_ref[box_ref[position]] = position
+        place = SKEL_ORDER.index(position // boxes) * boxes + position % boxes
+        place_ref[box_ref[position]] = place
     plain, other = [], []
     for k in range(boxes):
         rows = pl.ds(k * BOX, BOX)
@@ -64,6 +98,7 @@
 
 
 def mid_kernel(boxes, rank, parts_ref, expand_ref, response_ref):
+    strip = response_ref.shape[1]
     total = parts_ref[0].astype(jnp.float32)
     for source in range(1, parts_ref.shape[0]):
         total = total + parts_ref[source].astype(jnp.float32)
@@ -73,9 +108,12 @@
         stacked = jnp.concatenate([owned, turned(owned)], axis=0).astype(jnp.bfloat16)
         for start in range(k * BOX, (k + 1) * BOX, CHUNK):
             rows = pl.ds(start, CHUNK)
-            response_ref[rows, :] = jnp.dot(
+            response = jnp.dot(
                 expand_ref[rows, :], stacked, preferred_element_type=jnp.float32
             ).astype(jnp.bfloat16)
+            for part in range(CHUNK // strip):
+                place = FREQ_ORDER.index(start // strip + part)
+                response_ref[place] = response[part * strip : (part + 1) * strip]
 
 
 def on_device(incident, compress, coupling, expand, box_list, spectrum, *, freqs, skels):
@@ -94,16 +132,15 @@
         name="front",
     )(box_list, compress[0], incident[0], coupling[0])
     sent = sent.reshape(skels, all_rows // skels, columns)
-    parts = lax.all_to_all(sent, "skel", split_axis=0, concat_axis=0, tiled=True)
+    parts = lax.all_to_all(sent, SKEL_WALK, split_axis=0, concat_axis=0, tiled=True)
     response = pl.pallas_call(
         functools.partial(mid_kernel, boxes, rank),
-        out_shape=jax.ShapeDtypeStruct((local_rows, columns), jnp.bfloat16),
+        out_shape=jax.ShapeDtypeStruct((freqs, local_rows // freqs, columns), jnp.bfloat16),
         in_specs=[vmem, vmem],
         out_specs=vmem,
         name="mid", compiler_params=pltpu.CompilerParams(vmem_limit_bytes=SMALL_GRANT),
     )(parts, expand[0])
-    response = response.reshape(freqs, local_rows // freqs, columns)
-    spaced = lax.all_to_all(response, "freq", split_axis=0, concat_axis=0, tiled=True)
+    spaced = lax.all_to_all(response, FREQ_WALK, split_axis=0, concat_axis=0, tiled=True)
     traces = jnp.einsum(
         "fnca,cft->nat",
         spaced.reshape(freqs, local_rows // freqs, 2, angles),
@@ -114,11 +151,12 @@
 
 
 def solution(mesh):
+    chips = Mesh(mesh.devices.reshape(FREQ_SIZES + SKEL_SIZES), FREQ_AXES + SKEL_AXES)
     placed = (
-        P("freq", "skel", None),
-        P("freq", "skel", None),
-        P("freq", None, None, "skel"),
-        P("freq", "skel", None),
+        P(FREQ_AXES, SKEL_AXES, None),
+        P(FREQ_AXES, SKEL_AXES, None),
+        P(FREQ_AXES, None, None, SKEL_AXES),
+        P(FREQ_AXES, SKEL_AXES, None),
         P(),
         P(),
     )
@@ -128,8 +166,8 @@
 
     return jax.shard_map(
         body,
-        mesh=mesh,
+        mesh=chips,
         in_specs=placed,
-        out_specs=P(("skel", "freq"), None, None),
+        out_specs=P(SKEL_AXES + FREQ_AXES, None, None),
         check_vma=False,
     )

time: 81.5 us -> 78.9 us (0.968)
  the two profiles are of different devices: /device:TPU:33 before, /device:TPU:41 now
where the time goes in v3:
time: 78.9 us; the launch traced here: 78.6 us
  waiting for transfers between devices  32.8 us (42%)
  blocking collectives  20.1 us (25%)
  starting transfers between devices  17.7 us (22%)
  Pallas kernels  4.47 us (6%)
  matrix products  2.45 us (3%)
    all_to_all x1, waiting for transfers between devices, on_device(): lax.all_to_all(response, FREQ_WALK, split_axis=0, concat_axis=0, tiled=True)  32.8 us
    all_to_all x1, blocking collectives, on_device(): lax.all_to_all(sent, SKEL_WALK, split_axis=0, concat_axis=0, tiled=True)  20.1 us
    all_to_all x1, starting transfers between devices, on_device(): lax.all_to_all(response, FREQ_WALK, split_axis=0, concat_axis=0, tiled=True)  17.7 us
    pallas_call x1, Pallas kernels, on_device(): pl.pallas_call(functools.partial(front_kernel, boxes, rank), out_shape=ja...  3.29 us
    dot_general x1, matrix products, on_device(): jnp.einsum('fnca,cft->nat', spaced.reshape(freqs, local_rows // freqs, 2,...  2.45 us
  transfers between devices with their start and end apart: 1, of which 1 were waited for; matrix products, arithmetic and copies ran while one was open for 1% of the time, Pallas kernels for 0%

profile of v3, /device:TPU:41, one launch (start us, length us, event | category | flops | bytes accessed | tf_op | source)
XLA Modules:
  0.0 78.6 jit_solution(7241287765649741088)
XLA Ops:
  0.0 0.0 copy-start
  0.0 3.3 %front.1 = bf16[2048,128]{1,0:T(8,128)(2,1)} custom-call(s32[32]{0:T(128)} %box_ref.1, bf16[2048,128]{1,0:T(8,128)(2,1)} %bitcast.15, bf16[2048,128]{1,0:T(8,128)(2,1)} %bitcast.16, bf16[2,2048,128]{2,1,0:T(8,128)(2,1)} %bitcast.14), custom_call_target="tpu_custom_call" | custom-call | tf_op jit(solution)/shard_map/front/pallas_call | solution.py:126
  3.3 0.0 copy-start.1
  3.3 20.1 %all_to_all.10.parts_ref = bf16[16,128,128]{2,1,0:T(8,128)(2,1)S(1)} all-to-all(bf16[16,128,128]{2,1,0:T(8,128)(2,1)} %bitcast.13), channel_id=1, replica_groups=mesh['x'=4,'far'=4,'core'=2,'near'=4,'y'=4] {'y','near'}, dimensions={0} | all-to-all | bytes 1048576 | tf_op jit(solution)/shard_map/all_to_all | solution.py:135
  23.4 0.0 copy-done
  23.4 1.2 %mid.1 = bf16[32,64,128]{2,1,0:T(8,128)(2,1)} custom-call(bf16[16,128,128]{2,1,0:T(8,128)(2,1)S(1)} %all_to_all.10.parts_ref, bf16[2048,128]{1,0:T(8,128)(2,1)S(1)} %bitcast.12), custom_call_target="tpu_custom_call" | custom-call | tf_op jit(solution)/shard_map/mid/pallas_call | solution.py:136
  24.6 17.7 %all-to-all-start.1 = ((bf16[32,64,128]{2,1,0:T(8,128)(2,1)}), bf16[32,64,128]{2,1,0:T(8,128)(2,1)S(1)}, u32[]{:S(2)}, u32[]{:S(2)}) async-start(bf16[32,64,128]{2,1,0:T(8,128)(2,1)} %mid.1), calls=%async_computation.1 | async-start | bytes 1048576 | tf_op jit(solution)/shard_map/all_to_all | solution.py:143
  42.3 0.1 add.54
  42.4 0.0 copy-done.1
  42.4 0.1 reshape.219
  42.5 0.1 copy.9
  42.6 0.1 mul.81
  42.7 0.2 multiply_convert_fusion.1
  42.9 32.8 %all-to-all-done.1 = bf16[32,64,128]{2,1,0:T(8,128)(2,1)S(1)} async-done(((bf16[32,64,128]{2,1,0:T(8,128)(2,1)}), bf16[32,64,128]{2,1,0:T(8,128)(2,1)S(1)}, u32[]{:S(2)}, u32[]{:S(2)}) %all-to-all-start.1) | async-done | bytes 524320 | tf_op jit(solution)/shard_map/all_to_all | solution.py:143
  75.8 0.4 reshape.218
  76.2 2.4 %bitcast_convert_fusion = bf16[64,64,256]{2,1,0:T(8,128)(2,1)} fusion(bf16[32,64,2,64]{3,2,1,0:T(2,128)(2,1)S(1)} %reshape.218, bf16[1,32,256]{2,1,0:T(8,128)(2,1)S(1)} %get-tuple-element.6, bf16[1,32,256]{2,1,0:T(8,128)(2,1)S(1)} %get-tuple-element.5), kind=kOutput, calls=%fused_computation | convolution fusion | flops 135282688 | bytes 2654208 | tf_op jit(solution)/shard_map/fnca,cft->nat/dot_general | solution.py:144
  (2 shorter events, 0.0 us)
Async XLA Ops:
  0.0 23.4 %copy-start = (bf16[1,2048,128]{2,1,0:T(8,128)(2,1)S(1)}, bf16[1,2048,128]{2,1,0:T(8,128)(2,1)}, u32[]{:S(2)}) copy-start(bf16[1,2048,128]{2,1,0:T(8,128)(2,1)} %param.9) | copy-start | bytes 1572868
  3.3 39.1 %copy-start.1 = (f32[32]{0:T(128)S(1)}, f32[32]{0:T(128)}, u32[]{:S(2)}) copy-start(f32[32]{0:T(128)} %param.11) | copy-start | bytes 388
  24.6 51.1 %all-to-all-start.1 = ((bf16[32,64,128]{2,1,0:T(8,128)(2,1)}), bf16[32,64,128]{2,1,0:T(8,128)(2,1)S(1)}, u32[]{:S(2)}, u32[]{:S(2)}) async-start(bf16[32,64,128]{2,1,0:T(8,128)(2,1)} %mid.1), calls=%async_computation.1 | async-start | bytes 1048576 | tf_op jit(solution)/shard_map/all_to_all | solution.py:143
